TPU v7x, 32 devices: a whole 2x2x4 slice. The times are simulated.
32 devices in a mesh: sx: 8 (over y, x, core), sy: 4 (over z).
Axes of the slice: x: 2, y: 2, z: 4, core: 2. Of those that a mesh axis runs over, the one named last changes fastest.
Arguments:
- adjoint_loads: float32 [8, 8, 2, 288, 128], P('sx', 'sy'), may hold values from -6 to 6
- dual_taut: bfloat16 [8, 8, 1152, 1152], P('sx', 'sy'), may hold values from -1 to 2
- dual_wrinkle: bfloat16 [8, 8, 1152, 1152], P('sx', 'sy'), may hold values from -1 to 2
- dirichlet_taut: bfloat16 [8, 8, 1152, 1152], P('sx', 'sy'), may hold values from -1 to 2
- dirichlet_wrinkle: bfloat16 [8, 8, 1152, 1152], P('sx', 'sy'), may hold values from -1 to 2
- coupling: bfloat16 [8, 8, 12, 1152], P('sx', 'sy'), may hold values from -0.25 to 0.25
- coarse_inverse: bfloat16 [256, 256], P('sx', 'sy'), may hold values from -1 to 2
- wrinkled: int32 [8, 8], P('sx', 'sy'), may hold values 0 or 1
- edge_lengths: int32 [8, 8, 2], P('sx', 'sy'), may hold values from 144 to 288
- corner_map: int32 [8, 8, 12], P('sx', 'sy'), may hold values from 0 to 255, as said below
Outputs:
- multipliers: float32 [8, 8, 2, 288, 128], P('sx', 'sy')
- preconditioned: float32 [8, 8, 2, 288, 128], P('sx', 'sy')
Inputs may be any that keep to these rules, and one draw needn't show every extreme that they name: `corner_map`: each subdomain names 12 distinct coarse indices, three for each of its four grid corners; subdomains that meet at a grid corner name the same three indices for it; distinct grid corners name distinct indices.
All inputs are finite; a program needn't handle non-finite values. No bound on the sum of `wrinkled` on one device may be relied on, other than what follows from the above.
Results may differ from a plain program's by a relative error of at most 0.012.
Values may be sent and summed in bfloat16 or wider, within the bound.
A program may use at most 64 MiB of HBM per device.

v0:
```python
import jax
import jax.numpy as jnp
from jax import lax
from jax.sharding import PartitionSpec as P

EDGE = 288
CORNERS = 12
ITERS = 2
step_sizes = (0.55, 0.75)
momenta = (0.0, 0.15)


def from_behind(shard, axis, by):
    peers = lax.axis_size(axis)
    pairs = [(i, i + by) for i in range(peers) if 0 <= i + by < peers]
    return lax.ppermute(shard, axis, pairs)


def edge_mask(edge_lengths):
    per_row = edge_lengths.shape[1]
    shape_all = (1, per_row, 2, EDGE)
    positions = lax.broadcasted_iota(jnp.int32, shape_all, 3)
    inside = positions < edge_lengths[:, :, :, None]
    columns = lax.axis_index("sy") * per_row + lax.broadcasted_iota(jnp.int32, shape_all, 1)
    edge_kind = lax.broadcasted_iota(jnp.int32, shape_all, 2)
    exists = jnp.where(
        edge_kind == 0,
        columns < per_row * lax.axis_size("sy") - 1,
        lax.axis_index("sx") < lax.axis_size("sx") - 1,
    )
    return (inside & exists).astype(jnp.float32)[..., None]


def spread(edges):
    east_edge = edges[:, :, 0]
    south_edge = edges[:, :, 1]
    from_left = from_behind(east_edge[:, -1:], "sy", 1)
    west_edge = jnp.concatenate([from_left, east_edge[:, :-1]], axis=1)
    north_edge = from_behind(south_edge, "sx", 1)
    return jnp.concatenate([east_edge, south_edge, -west_edge, -north_edge], axis=2)


def collect(local_part):
    west_part = local_part[:, :, 2 * EDGE : 3 * EDGE]
    from_right = from_behind(west_part[:, :1], "sy", -1)
    right_west = jnp.concatenate([west_part[:, 1:], from_right], axis=1)
    down_north = from_behind(local_part[:, :, 3 * EDGE :], "sx", -1)
    return jnp.stack(
        [local_part[:, :, :EDGE] - right_west, local_part[:, :, EDGE : 2 * EDGE] - down_north],
        axis=2,
    )


def paired(taut, wrinkle, wrinkled, vectors):
    base_part = jnp.einsum("rsij,rsjl->rsil", taut, vectors, preferred_element_type=jnp.float32)
    extra_part = jnp.einsum("rsij,rsjl->rsil", wrinkle, vectors, preferred_element_type=jnp.float32)
    return base_part + wrinkled.astype(jnp.float32)[:, :, None, None] * extra_part


def coarse_term(coupling, corner_map, coarse_inverse, vectors):
    col_count = coarse_inverse.shape[1]
    coarse_order = col_count * lax.axis_size("sy")
    corner_terms = jnp.einsum(
        "rskj,rsjl->rskl", coupling, vectors, preferred_element_type=jnp.float32
    )
    corner_terms = corner_terms.reshape(-1, corner_terms.shape[-1])
    corner_index = corner_map.reshape(-1)
    selector = corner_index[:, None] == lax.broadcasted_iota(
        jnp.int32, (corner_index.shape[0], coarse_order), 1
    )
    selector_float = selector.astype(jnp.float32)
    placed = jnp.einsum("kc,kl->cl", selector_float, corner_terms, precision=lax.Precision.HIGHEST)
    totals = lax.psum(placed, ("sx", "sy"))
    column_part = lax.dynamic_slice_in_dim(totals, lax.axis_index("sy") * col_count, col_count, 0)
    row_part = jnp.dot(
        coarse_inverse, column_part.astype(jnp.bfloat16), preferred_element_type=jnp.float32
    )
    solved = lax.psum(row_part, "sy").astype(jnp.bfloat16)
    selector_half = selector.astype(jnp.bfloat16)
    selected = jnp.dot(
        selector_half,
        lax.all_gather(solved, "sx", axis=0, tiled=True),
        preferred_element_type=jnp.float32,
    )
    selected = selected.astype(jnp.bfloat16).reshape(
        vectors.shape[0], vectors.shape[1], CORNERS, -1
    )
    return jnp.einsum("rskj,rskl->rsjl", coupling, selected, preferred_element_type=jnp.float32)


def local(
    adjoint_loads,
    dual_taut,
    dual_wrinkle,
    dirichlet_taut,
    dirichlet_wrinkle,
    coupling,
    coarse_inverse,
    wrinkled,
    edge_lengths,
    corner_map,
):
    masking = edge_mask(edge_lengths)
    loads = adjoint_loads * masking

    def precondition(incoming):
        vectors = spread((0.5 * incoming).astype(jnp.bfloat16))
        return 0.5 * collect(paired(dirichlet_taut, dirichlet_wrinkle, wrinkled, vectors)) * masking

    multipliers = jnp.zeros_like(loads)
    direction = jnp.zeros_like(loads)
    residual = loads
    for number in range(ITERS):
        direction = precondition(residual) + momenta[number] * direction
        multipliers = multipliers + step_sizes[number] * direction
        dual_vectors = spread(multipliers.astype(jnp.bfloat16))
        local_part = paired(dual_taut, dual_wrinkle, wrinkled, dual_vectors)
        local_part = local_part + coarse_term(coupling, corner_map, coarse_inverse, dual_vectors)
        residual = loads - collect(local_part) * masking
    return (multipliers, precondition(residual))


def solution(mesh):
    placed = (
        P("sx", "sy", None, None, None),
        P("sx", "sy", None, None),
        P("sx", "sy", None, None),
        P("sx", "sy", None, None),
        P("sx", "sy", None, None),
        P("sx", "sy", None, None),
        P("sx", "sy"),
        P("sx", "sy"),
        P("sx", "sy", None),
        P("sx", "sy", None),
    )
    return jax.shard_map(
        local,
        mesh=mesh,
        in_specs=placed,
        out_specs=(P("sx", "sy", None, None, None), P("sx", "sy", None, None, None)),
        check_vma=False,
    )
```

profile of v0, /device:TPU:1, one launch (start us, length us, event | category | flops | bytes accessed | tf_op | source)
XLA Modules:
  0.0 320.2 jit_solution(4290553914124060883)
XLA Ops:
  1.4 1.3 copy.33
  3.0 4.0 %collective-permute-start = (bf16[1,1,288,128]{2,3,1,0:T(8,128)(2,1)S(1)}, bf16[1,1,288,128]{2,3,1,0:T(8,128)(2,1)S(1)}, u32[]{:S(2)}, u32[]{:S(2)}) collective-permute-start(bf16[1,1,288,128]{2,3,1,0:T(8,128)(2,1)S(1)} %get-tuple-element.48), channel_id=1, source_target_pairs={{0,1},{1,2},{2,3},{4,5},{5,6},{6,7},{8,9},{9,10},{10,11},{12,13},{... | collective-permute-start | bytes 221192 | tf_op jit(solution)/shard_map/ppermute | solution.py:16
  7.0 4.0 %collective-permute-start.1 = (bf16[1,2,288,128]{2,3,1,0:T(8,128)(2,1)S(1)}, bf16[1,2,288,128]{2,3,1,0:T(8,128)(2,1)S(1)}, u32[]{:S(2)}, u32[]{:S(2)}) collective-permute-start(bf16[1,2,288,128]{2,3,1,0:T(8,128)(2,1)S(1)} %get-tuple-element.38), channel_id=1, source_target_pairs={{0,4},{4,8},{8,12},{12,16},{16,20},{20,24},{24,28},{1,5},{5,9},{9,... | collective-permute-start | bytes 442376 | tf_op jit(solution)/shard_map/ppermute | solution.py:16
  11.1 2.5 collective-permute-done.1
  14.2 4.3 %fusion.29 = f32[2,128,1152]{2,1,0:T(8,128)S(1)} fusion(bf16[1,2,1152,1152]{3,2,1,0:T(8,128)(2,1)} %param.14, bf16[1,2,1152,128]{2,3,1,0:T(8,128)(2,1)S(1)} %concatenate.138, f32[2]{0:T(128)S(1)} %convert_bitcast_fusion), kind=kOutput, calls=%fused_computation.23 | convolution fusion | flops 679772160 | bytes 7077896 | tf_op jit(solution)/shard_map/rsij,rsjl->rsil/dot_general | solution.py:56
  18.6 1.7 fusion.68
  21.8 5.1 %collective-permute-done.2 = f32[1,1,288,128]{2,3,1,0:T(8,128)S(1)} collective-permute-done((f32[1,1,288,128]{2,3,1,0:T(8,128)S(1)}, f32[1,1,288,128]{2,3,1,0:T(8,128)S(1)}, u32[]{:S(2)}, u32[]{:S(2)}) %collective-permute-start.2) | collective-permute-done | bytes 147488 | tf_op jit(solution)/shard_map/ppermute | solution.py:16
  27.1 1.9 collective-permute-start.3
  29.1 9.2 %collective-permute-done.3 = f32[1,2,288,128]{2,3,1,0:T(8,128)S(1)} collective-permute-done((f32[1,2,288,128]{2,3,1,0:T(8,128)S(1)}, f32[1,2,288,128]{2,3,1,0:T(8,128)S(1)}, u32[]{:S(2)}, u32[]{:S(2)}) %collective-permute-start.3) | collective-permute-done | bytes 294944 | tf_op jit(solution)/shard_map/ppermute | solution.py:16
  39.3 3.2 collective-permute-start.4
  42.5 2.0 collective-permute-start.5
  47.9 1.4 concatenate.141
  50.0 41.2 %all-reduce.2 = bf16[256,128]{1,0:T(8,128)(2,1)S(1)} all-reduce(f32[256,128]{1,0:T(8,128)S(1)} %fusion.109), channel_id=1, replica_groups=mesh['sx'=8,'sy'=4] {'sx','sy'}, use_global_device_ids=true, to_apply=%region_0.1 | all-reduce | flops 32768 | bytes 196608 | tf_op jit(solution)/shard_map/psum | solution.py:73
  92.1 13.2 %psum.29 = bf16[32,128]{1,0:T(8,128)(2,1)S(1)} all-reduce(f32[32,128]{1,0:T(8,128)S(1)} %convolution_bitcast_fusion.1), channel_id=1, replica_groups=mesh['sx'=8,'sy'=4] {'sy'}, use_global_device_ids=true, to_apply=%region_1.2 | all-reduce | flops 4096 | bytes 24576 | tf_op jit(solution)/shard_map/psum | solution.py:78
  105.2 15.1 %all_gather.6 = bf16[256,128]{1,0:T(8,128)(2,1)S(1)} all-gather(bf16[32,128]{1,0:T(8,128)(2,1)S(1)} %psum.29), channel_id=1, replica_groups=mesh['sx'=8,'sy'=4] {'sx'}, dimensions={0}, use_global_device_ids=true | all-gather | bytes 73728 | tf_op jit(solution)/shard_map/all_gather | solution.py:82
  120.9 4.4 %fusion.44 = f32[2,128,1152]{2,1,0:T(8,128)S(1)} fusion(bf16[1,2,1152,1152]{3,2,1,0:T(8,128)(2,1)} %param.12, bf16[1,2,1152,128]{2,3,1,0:T(8,128)(2,1)S(1)} %concatenate.141, f32[2]{0:T(128)S(1)} %convert_bitcast_fusion), kind=kOutput, calls=%fused_computation.28 | convolution fusion | flops 679772160 | bytes 7077896 | tf_op jit(solution)/shard_map/rsij,rsjl->rsil/dot_general | solution.py:56
  125.3 1.7 fusion.56
  128.5 6.9 %collective-permute-done.6 = f32[1,1,288,128]{2,3,1,0:T(8,128)S(1)} collective-permute-done((f32[1,1,288,128]{2,3,1,0:T(8,128)S(1)}, f32[1,1,288,128]{2,3,1,0:T(8,128)S(1)}, u32[]{:S(2)}, u32[]{:S(2)}) %collective-permute-start.6) | collective-permute-done | bytes 147488 | tf_op jit(solution)/shard_map/ppermute | solution.py:16
  135.6 2.9 collective-permute-start.7
  138.5 7.0 %collective-permute-done.7 = f32[1,2,288,128]{2,3,1,0:T(8,128)S(1)} collective-permute-done((f32[1,2,288,128]{2,3,1,0:T(8,128)S(1)}, f32[1,2,288,128]{2,3,1,0:T(8,128)S(1)}, u32[]{:S(2)}, u32[]{:S(2)}) %collective-permute-start.7) | collective-permute-done | bytes 294944 | tf_op jit(solution)/shard_map/ppermute | solution.py:16
  145.9 1.5 collective-permute-start.8
  147.4 1.9 collective-permute-start.9
  149.4 2.5 collective-permute-done.9
  152.5 4.2 %fusion.32 = f32[2,128,1152]{2,1,0:T(8,128)S(1)} fusion(bf16[1,2,1152,1152]{3,2,1,0:T(8,128)(2,1)} %param.14, bf16[1,2,1152,128]{2,3,1,0:T(8,128)(2,1)S(1)} %concatenate.144, f32[2]{0:T(128)S(1)} %convert_bitcast_fusion), kind=kOutput, calls=%fused_computation.24 | convolution fusion | flops 679772160 | bytes 7077896 | tf_op jit(solution)/shard_map/rsij,rsjl->rsil/dot_general | solution.py:56
  156.7 4.2 %fusion.65 = f32[1,2,1152,128]{2,3,1,0:T(8,128)S(1)} fusion(f32[2,128,1152]{2,1,0:T(8,128)S(1)} %fusion.32, bf16[1,2,1152,1152]{3,2,1,0:T(8,128)(2,1)} %param.13, bf16[1,2,1152,128]{2,3,1,0:T(8,128)(2,1)S(1)} %concatenate.144), kind=kOutput, calls=%fused_computation.35 | convolution fusion | flops 679772160 | bytes 8257536 | tf_op jit(solution)/shard_map/rsij,rsjl->rsil/dot_general | solution.py:55
  162.4 6.6 %collective-permute-done.10 = f32[1,1,288,128]{2,3,1,0:T(8,128)S(1)} collective-permute-done((f32[1,1,288,128]{2,3,1,0:T(8,128)S(1)}, f32[1,1,288,128]{2,3,1,0:T(8,128)S(1)}, u32[]{:S(2)}, u32[]{:S(2)}) %collective-permute-start.10) | collective-permute-done | bytes 147488 | tf_op jit(solution)/shard_map/ppermute | solution.py:16
  169.2 2.1 collective-permute-start.11
  171.3 8.1 %collective-permute-done.11 = f32[1,2,288,128]{2,3,1,0:T(8,128)S(1)} collective-permute-done((f32[1,2,288,128]{2,3,1,0:T(8,128)S(1)}, f32[1,2,288,128]{2,3,1,0:T(8,128)S(1)}, u32[]{:S(2)}, u32[]{:S(2)}) %collective-permute-start.11) | collective-permute-done | bytes 294944 | tf_op jit(solution)/shard_map/ppermute | solution.py:16
  180.8 2.5 collective-permute-start.12
  183.4 1.9 collective-permute-start.13
  185.4 2.5 collective-permute-done.13
  188.8 4.2 %fusion.47 = f32[2,128,1152]{2,1,0:T(8,128)S(1)} fusion(bf16[1,2,1152,1152]{3,2,1,0:T(8,128)(2,1)} %param.12, bf16[1,2,1152,128]{2,3,1,0:T(8,128)(2,1)S(1)} %concatenate.147, f32[2]{0:T(128)S(1)} %convert_bitcast_fusion), kind=kOutput, calls=%fused_computation.29 | convolution fusion | flops 679772160 | bytes 7077896 | tf_op jit(solution)/shard_map/rsij,rsjl->rsil/dot_general | solution.py:56
  193.4 39.6 %all-reduce.3 = bf16[256,128]{1,0:T(8,128)(2,1)S(1)} all-reduce(f32[256,128]{1,0:T(8,128)S(1)} %fusion.108), channel_id=1, replica_groups=mesh['sx'=8,'sy'=4] {'sx','sy'}, use_global_device_ids=true, to_apply=%region_2.3 | all-reduce | flops 32768 | bytes 196608 | tf_op jit(solution)/shard_map/psum | solution.py:73
  233.2 13.5 %psum.31 = bf16[32,128]{1,0:T(8,128)(2,1)S(1)} all-reduce(f32[32,128]{1,0:T(8,128)S(1)} %convolution_bitcast_fusion), channel_id=1, replica_groups=mesh['sx'=8,'sy'=4] {'sy'}, use_global_device_ids=true, to_apply=%region_3.4 | all-reduce | flops 4096 | bytes 24576 | tf_op jit(solution)/shard_map/psum | solution.py:78
  246.7 15.0 %all_gather.7 = bf16[256,128]{1,0:T(8,128)(2,1)S(1)} all-gather(bf16[32,128]{1,0:T(8,128)(2,1)S(1)} %psum.31), channel_id=1, replica_groups=mesh['sx'=8,'sy'=4] {'sx'}, dimensions={0}, use_global_device_ids=true | all-gather | bytes 73728 | tf_op jit(solution)/shard_map/all_gather | solution.py:82
  262.3 4.2 %fusion.59 = f32[1,2,1152,128]{2,3,1,0:T(8,128)S(1)} fusion(f32[2,128,1152]{2,1,0:T(8,128)S(1)} %fusion.102, f32[2,128,1152]{2,1,0:T(8,128)S(1)} %fusion.47, bf16[1,2,1152,1152]{3,2,1,0:T(8,128)(2,1)} %param.11, bf16[1,2,1152,128]{2,3,1,0:T(8,128)(2,1)S(1)} %concatenate.147), kind=kOutput, calls=%fused_computation.33 | convolution fusion | flops 680067072 | bytes 9437184 | tf_op jit(solution)/shard_map/rsij,rsjl->rsil/dot_general | solution.py:55
  268.0 6.9 %collective-permute-done.14 = f32[1,1,288,128]{2,3,1,0:T(8,128)S(1)} collective-permute-done((f32[1,1,288,128]{2,3,1,0:T(8,128)S(1)}, f32[1,1,288,128]{2,3,1,0:T(8,128)S(1)}, u32[]{:S(2)}, u32[]{:S(2)}) %collective-permute-start.14) | collective-permute-done | bytes 147488 | tf_op jit(solution)/shard_map/ppermute | solution.py:16
  275.0 2.9 collective-permute-start.15
  278.0 7.0 %collective-permute-done.15 = f32[1,2,288,128]{2,3,1,0:T(8,128)S(1)} collective-permute-done((f32[1,2,288,128]{2,3,1,0:T(8,128)S(1)}, f32[1,2,288,128]{2,3,1,0:T(8,128)S(1)}, u32[]{:S(2)}, u32[]{:S(2)}) %collective-permute-start.15) | collective-permute-done | bytes 294944 | tf_op jit(solution)/shard_map/ppermute | solution.py:16
  285.4 1.5 collective-permute-start.16
  286.9 1.9 collective-permute-start.17
  288.9 2.5 collective-permute-done.17
  292.0 4.2 %fusion.35 = f32[2,128,1152]{2,1,0:T(8,128)S(1)} fusion(bf16[1,2,1152,1152]{3,2,1,0:T(8,128)(2,1)} %param.14, bf16[1,2,1152,128]{2,3,1,0:T(8,128)(2,1)S(1)} %concatenate.150, f32[2]{0:T(128)S(1)} %convert_bitcast_fusion), kind=kOutput, calls=%fused_computation.25 | convolution fusion | flops 679772160 | bytes 7077896 | tf_op jit(solution)/shard_map/rsij,rsjl->rsil/dot_general | solution.py:56
  296.2 4.2 %fusion.62 = f32[1,2,1152,128]{2,3,1,0:T(8,128)S(1)} fusion(f32[2,128,1152]{2,1,0:T(8,128)S(1)} %fusion.35, bf16[1,2,1152,1152]{3,2,1,0:T(8,128)(2,1)} %param.13, bf16[1,2,1152,128]{2,3,1,0:T(8,128)(2,1)S(1)} %concatenate.150), kind=kOutput, calls=%fused_computation.34 | convolution fusion | flops 679772160 | bytes 8257536 | tf_op jit(solution)/shard_map/rsij,rsjl->rsil/dot_general | solution.py:55
  300.6 1.4 collective-permute-start.18
  302.0 6.6 %collective-permute-done.18 = f32[1,1,288,128]{2,3,1,0:T(8,128)S(1)} collective-permute-done((f32[1,1,288,128]{2,3,1,0:T(8,128)S(1)}, f32[1,1,288,128]{2,3,1,0:T(8,128)S(1)}, u32[]{:S(2)}, u32[]{:S(2)}) %collective-permute-start.18) | collective-permute-done | bytes 147488 | tf_op jit(solution)/shard_map/ppermute | solution.py:16
  308.8 2.0 collective-permute-start.19
  311.9 7.0 %collective-permute-done.19 = f32[1,2,288,128]{2,3,1,0:T(8,128)S(1)} collective-permute-done((f32[1,2,288,128]{2,3,1,0:T(8,128)S(1)}, f32[1,2,288,128]{2,3,1,0:T(8,128)S(1)}, u32[]{:S(2)}, u32[]{:S(2)}) %collective-permute-start.19) | collective-permute-done | bytes 294944 | tf_op jit(solution)/shard_map/ppermute | solution.py:16
  (94 shorter events, 22.7 us)
Async XLA Ops:
  0.6 48.7 %copy-start = (bf16[1,2,12,1152]{3,1,2,0:T(2,128)(2,1)S(1)}, bf16[1,2,12,1152]{3,1,2,0:T(2,128)(2,1)}, u32[]{:S(2)}) copy-start(bf16[1,2,12,1152]{3,1,2,0:T(2,128)(2,1)} %param.15) | copy-start | bytes 165892
  2.8 8.2 %copy-start.5 = (s32[1,2]{1,0:T(1,128)S(1)}, s32[1,2]{1,0:T(1,128)}, u32[]{:S(2)}) copy-start(s32[1,2]{1,0:T(1,128)} %param.17) | copy-start | bytes 28
  3.0 8.0 %collective-permute-start = (bf16[1,1,288,128]{2,3,1,0:T(8,128)(2,1)S(1)}, bf16[1,1,288,128]{2,3,1,0:T(8,128)(2,1)S(1)}, u32[]{:S(2)}, u32[]{:S(2)}) collective-permute-start(bf16[1,1,288,128]{2,3,1,0:T(8,128)(2,1)S(1)} %get-tuple-element.48), channel_id=1, source_target_pairs={{0,1},{1,2},{2,3},{4,5},{5,6},{6,7},{8,9},{9,10},{10,11},{12,13},{... | collective-permute-start | bytes 221192 | tf_op jit(solution)/shard_map/ppermute | solution.py:16
  7.0 6.6 %collective-permute-start.1 = (bf16[1,2,288,128]{2,3,1,0:T(8,128)(2,1)S(1)}, bf16[1,2,288,128]{2,3,1,0:T(8,128)(2,1)S(1)}, u32[]{:S(2)}, u32[]{:S(2)}) collective-permute-start(bf16[1,2,288,128]{2,3,1,0:T(8,128)(2,1)S(1)} %get-tuple-element.38), channel_id=1, source_target_pairs={{0,4},{4,8},{8,12},{12,16},{16,20},{20,24},{24,28},{1,5},{5,9},{9,... | collective-permute-start | bytes 442376 | tf_op jit(solution)/shard_map/ppermute | solution.py:16
  14.2 4.4 %copy-start.1 = (bf16[1,2,1152,1152]{3,2,1,0:T(8,128)(2,1)S(1)}, bf16[1,2,1152,1152]{3,2,1,0:T(8,128)(2,1)}, u32[]{:S(2)}) copy-start(bf16[1,2,1152,1152]{3,2,1,0:T(8,128)(2,1)} %param.13) | copy-start | bytes 15925252
  20.5 6.4 %collective-permute-start.2 = (f32[1,1,288,128]{2,3,1,0:T(8,128)S(1)}, f32[1,1,288,128]{2,3,1,0:T(8,128)S(1)}, u32[]{:S(2)}, u32[]{:S(2)}) collective-permute-start(f32[1,1,288,128]{2,3,1,0:T(8,128)S(1)} %get-tuple-element.29), channel_id=1, source_target_pairs={{1,0},{2,1},{3,2},{5,4},{6,5},{7,6},{9,8},{10,9},{11,10},{13,12},{... | collective-permute-start | bytes 442376 | tf_op jit(solution)/shard_map/ppermute | solution.py:16
  27.1 11.3 %collective-permute-start.3 = (f32[1,2,288,128]{2,3,1,0:T(8,128)S(1)}, f32[1,2,288,128]{2,3,1,0:T(8,128)S(1)}, u32[]{:S(2)}, u32[]{:S(2)}) collective-permute-start(f32[1,2,288,128]{2,3,1,0:T(8,128)S(1)} %get-tuple-element.27), channel_id=1, source_target_pairs={{4,0},{8,4},{12,8},{16,12},{20,16},{24,20},{28,24},{5,1},{9,5},{13... | collective-permute-start | bytes 884744 | tf_op jit(solution)/shard_map/ppermute | solution.py:16
  38.5 86.8 %slice-start = ((s8[5308416]{0:T(1024)(128)(4,1)}), s8[1114112]{0:T(1024)(128)(4,1)S(1)}, s32[]{:S(2)}) async-start(s8[5308416]{0:T(1024)(128)(4,1)} %bitcast.171), calls=%async_computation | async-start | bytes 2228224
  38.6 8.5 %copy-start.3 = (bf16[1,2,288,128]{2,3,1,0:T(8,128)(2,1)}, bf16[1,2,288,128]{2,3,1,0:T(8,128)(2,1)S(1)}, u32[]{:S(2)}) copy-start(bf16[1,2,288,128]{2,3,1,0:T(8,128)(2,1)S(1)} %get-tuple-element.36) | copy-start | bytes 442372
  39.3 6.0 %collective-permute-start.4 = (bf16[1,1,288,128]{2,3,1,0:T(8,128)(2,1)}, bf16[1,1,288,128]{2,3,1,0:T(8,128)(2,1)S(1)}, u32[]{:S(2)}, u32[]{:S(2)}) collective-permute-start(bf16[1,1,288,128]{2,3,1,0:T(8,128)(2,1)} %get-tuple-element.46), channel_id=1, source_target_pairs={{0,1},{1,2},{2,3},{4,5},{5,6},{6,7},{8,9},{9,10},{10,11},{12,13},{... | collective-permute-start | bytes 221192 | tf_op jit(solution)/shard_map/ppermute | solution.py:16
  42.5 4.6 %collective-permute-start.5 = (bf16[1,2,288,128]{2,3,1,0:T(8,128)(2,1)S(1)}, bf16[1,2,288,128]{2,3,1,0:T(8,128)(2,1)S(1)}, u32[]{:S(2)}, u32[]{:S(2)}) collective-permute-start(bf16[1,2,288,128]{2,3,1,0:T(8,128)(2,1)S(1)} %get-tuple-element.36), channel_id=1, source_target_pairs={{0,4},{4,8},{8,12},{12,16},{16,20},{20,24},{24,28},{1,5},{5,9},{9,... | collective-permute-start | bytes 442376 | tf_op jit(solution)/shard_map/ppermute | solution.py:16
  120.5 4.8 %slice-start.1 = ((s8[5308416]{0:T(1024)(128)(4,1)}), s8[4194304]{0:T(1024)(128)(4,1)S(1)}, s32[]{:S(2)}) async-start(s8[5308416]{0:T(1024)(128)(4,1)} %bitcast.171), calls=%async_computation.1 | async-start | bytes 8388608
  127.2 8.2 %collective-permute-start.6 = (f32[1,1,288,128]{2,3,1,0:T(8,128)S(1)}, f32[1,1,288,128]{2,3,1,0:T(8,128)S(1)}, u32[]{:S(2)}, u32[]{:S(2)}) collective-permute-start(f32[1,1,288,128]{2,3,1,0:T(8,128)S(1)} %get-tuple-element.25), channel_id=1, source_target_pairs={{1,0},{2,1},{3,2},{5,4},{6,5},{7,6},{9,8},{10,9},{11,10},{13,12},{... | collective-permute-start | bytes 442376 | tf_op jit(solution)/shard_map/ppermute | solution.py:16
  135.6 9.9 %collective-permute-start.7 = (f32[1,2,288,128]{2,3,1,0:T(8,128)S(1)}, f32[1,2,288,128]{2,3,1,0:T(8,128)S(1)}, u32[]{:S(2)}, u32[]{:S(2)}) collective-permute-start(f32[1,2,288,128]{2,3,1,0:T(8,128)S(1)} %get-tuple-element.23), channel_id=1, source_target_pairs={{4,0},{8,4},{12,8},{16,12},{20,16},{24,20},{28,24},{5,1},{9,5},{13... | collective-permute-start | bytes 884744 | tf_op jit(solution)/shard_map/ppermute | solution.py:16
  145.9 3.4 %collective-permute-start.8 = (bf16[1,1,288,128]{2,3,1,0:T(8,128)(2,1)S(1)}, bf16[1,1,288,128]{2,3,1,0:T(8,128)(2,1)S(1)}, u32[]{:S(2)}, u32[]{:S(2)}) collective-permute-start(bf16[1,1,288,128]{2,3,1,0:T(8,128)(2,1)S(1)} %get-tuple-element.44), channel_id=1, source_target_pairs={{0,1},{1,2},{2,3},{4,5},{5,6},{6,7},{8,9},{9,10},{10,11},{12,13},{... | collective-permute-start | bytes 221192 | tf_op jit(solution)/shard_map/ppermute | solution.py:16
  147.4 4.5 %collective-permute-start.9 = (bf16[1,2,288,128]{2,3,1,0:T(8,128)(2,1)S(1)}, bf16[1,2,288,128]{2,3,1,0:T(8,128)(2,1)S(1)}, u32[]{:S(2)}, u32[]{:S(2)}) collective-permute-start(bf16[1,2,288,128]{2,3,1,0:T(8,128)(2,1)S(1)} %get-tuple-element.34), channel_id=1, source_target_pairs={{0,4},{4,8},{8,12},{12,16},{16,20},{20,24},{24,28},{1,5},{5,9},{9,... | collective-permute-start | bytes 442376 | tf_op jit(solution)/shard_map/ppermute | solution.py:16
  161.1 7.9 %collective-permute-start.10 = (f32[1,1,288,128]{2,3,1,0:T(8,128)S(1)}, f32[1,1,288,128]{2,3,1,0:T(8,128)S(1)}, u32[]{:S(2)}, u32[]{:S(2)}) collective-permute-start(f32[1,1,288,128]{2,3,1,0:T(8,128)S(1)} %get-tuple-element.21), channel_id=1, source_target_pairs={{1,0},{2,1},{3,2},{5,4},{6,5},{7,6},{9,8},{10,9},{11,10},{13,12},{... | collective-permute-start | bytes 442376 | tf_op jit(solution)/shard_map/ppermute | solution.py:16
  169.2 10.3 %collective-permute-start.11 = (f32[1,2,288,128]{2,3,1,0:T(8,128)S(1)}, f32[1,2,288,128]{2,3,1,0:T(8,128)S(1)}, u32[]{:S(2)}, u32[]{:S(2)}) collective-permute-start(f32[1,2,288,128]{2,3,1,0:T(8,128)S(1)} %get-tuple-element.19), channel_id=1, source_target_pairs={{4,0},{8,4},{12,8},{16,12},{20,16},{24,20},{28,24},{5,1},{9,5},{13... | collective-permute-start | bytes 884744 | tf_op jit(solution)/shard_map/ppermute | solution.py:16
  180.8 4.5 %collective-permute-start.12 = (bf16[1,1,288,128]{2,3,1,0:T(8,128)(2,1)S(1)}, bf16[1,1,288,128]{2,3,1,0:T(8,128)(2,1)S(1)}, u32[]{:S(2)}, u32[]{:S(2)}) collective-permute-start(bf16[1,1,288,128]{2,3,1,0:T(8,128)(2,1)S(1)} %get-tuple-element.42), channel_id=1, source_target_pairs={{0,1},{1,2},{2,3},{4,5},{5,6},{6,7},{8,9},{9,10},{10,11},{12,13},{... | collective-permute-start | bytes 221192 | tf_op jit(solution)/shard_map/ppermute | solution.py:16
  183.4 4.5 %collective-permute-start.13 = (bf16[1,2,288,128]{2,3,1,0:T(8,128)(2,1)S(1)}, bf16[1,2,288,128]{2,3,1,0:T(8,128)(2,1)S(1)}, u32[]{:S(2)}, u32[]{:S(2)}) collective-permute-start(bf16[1,2,288,128]{2,3,1,0:T(8,128)(2,1)S(1)} %get-tuple-element.32), channel_id=1, source_target_pairs={{0,4},{4,8},{8,12},{12,16},{16,20},{20,24},{24,28},{1,5},{5,9},{9,... | collective-permute-start | bytes 442376 | tf_op jit(solution)/shard_map/ppermute | solution.py:16
  188.8 44.3 %copy-start.4 = (bf16[32,64]{1,0:T(8,128)(2,1)S(1)}, bf16[32,64]{1,0:T(8,128)(2,1)}, u32[]{:S(2)}) copy-start(bf16[32,64]{1,0:T(8,128)(2,1)} %param.16) | copy-start | bytes 12292
  266.7 8.2 %collective-permute-start.14 = (f32[1,1,288,128]{2,3,1,0:T(8,128)S(1)}, f32[1,1,288,128]{2,3,1,0:T(8,128)S(1)}, u32[]{:S(2)}, u32[]{:S(2)}) collective-permute-start(f32[1,1,288,128]{2,3,1,0:T(8,128)S(1)} %get-tuple-element.17), channel_id=1, source_target_pairs={{1,0},{2,1},{3,2},{5,4},{6,5},{7,6},{9,8},{10,9},{11,10},{13,12},{... | collective-permute-start | bytes 442376 | tf_op jit(solution)/shard_map/ppermute | solution.py:16
  275.0 9.9 %collective-permute-start.15 = (f32[1,2,288,128]{2,3,1,0:T(8,128)S(1)}, f32[1,2,288,128]{2,3,1,0:T(8,128)S(1)}, u32[]{:S(2)}, u32[]{:S(2)}) collective-permute-start(f32[1,2,288,128]{2,3,1,0:T(8,128)S(1)} %get-tuple-element.15), channel_id=1, source_target_pairs={{4,0},{8,4},{12,8},{16,12},{20,16},{24,20},{28,24},{5,1},{9,5},{13... | collective-permute-start | bytes 884744 | tf_op jit(solution)/shard_map/ppermute | solution.py:16
  285.4 3.4 %collective-permute-start.16 = (bf16[1,1,288,128]{2,3,1,0:T(8,128)(2,1)S(1)}, bf16[1,1,288,128]{2,3,1,0:T(8,128)(2,1)S(1)}, u32[]{:S(2)}, u32[]{:S(2)}) collective-permute-start(bf16[1,1,288,128]{2,3,1,0:T(8,128)(2,1)S(1)} %get-tuple-element.40), channel_id=1, source_target_pairs={{0,1},{1,2},{2,3},{4,5},{5,6},{6,7},{8,9},{9,10},{10,11},{12,13},{... | collective-permute-start | bytes 221192 | tf_op jit(solution)/shard_map/ppermute | solution.py:16
  286.9 4.5 %collective-permute-start.17 = (bf16[1,2,288,128]{2,3,1,0:T(8,128)(2,1)S(1)}, bf16[1,2,288,128]{2,3,1,0:T(8,128)(2,1)S(1)}, u32[]{:S(2)}, u32[]{:S(2)}) collective-permute-start(bf16[1,2,288,128]{2,3,1,0:T(8,128)(2,1)S(1)} %get-tuple-element.30), channel_id=1, source_target_pairs={{0,4},{4,8},{8,12},{12,16},{16,20},{20,24},{24,28},{1,5},{5,9},{9,... | collective-permute-start | bytes 442376 | tf_op jit(solution)/shard_map/ppermute | solution.py:16
  300.6 10.2 %copy-start.2 = (f32[1,2,2,288,128]{3,4,1,2,0:T(8,128)S(1)}, f32[1,2,2,288,128]{3,4,1,2,0:T(8,128)}, u32[]{:S(2)}) copy-start(f32[1,2,2,288,128]{3,4,1,2,0:T(8,128)} %get-tuple-element.9) | copy-start | bytes 1769476
  300.6 8.1 %collective-permute-start.18 = (f32[1,1,288,128]{2,3,1,0:T(8,128)S(1)}, f32[1,1,288,128]{2,3,1,0:T(8,128)S(1)}, u32[]{:S(2)}, u32[]{:S(2)}) collective-permute-start(f32[1,1,288,128]{2,3,1,0:T(8,128)S(1)} %get-tuple-element.13), channel_id=1, source_target_pairs={{1,0},{2,1},{3,2},{5,4},{6,5},{7,6},{9,8},{10,9},{11,10},{13,12},{... | collective-permute-start | bytes 442376 | tf_op jit(solution)/shard_map/ppermute | solution.py:16
  308.8 10.1 %collective-permute-start.19 = (f32[1,2,288,128]{2,3,1,0:T(8,128)S(1)}, f32[1,2,288,128]{2,3,1,0:T(8,128)S(1)}, u32[]{:S(2)}, u32[]{:S(2)}) collective-permute-start(f32[1,2,288,128]{2,3,1,0:T(8,128)S(1)} %get-tuple-element.11), channel_id=1, source_target_pairs={{4,0},{8,4},{12,8},{16,12},{20,16},{24,20},{28,24},{5,1},{9,5},{13... | collective-permute-start | bytes 884744 | tf_op jit(solution)/shard_map/ppermute | solution.py:16
where the time goes:
time: 321 us; the launch traced here: 320 us
  blocking collectives  138 us (43%)
  waiting for transfers between devices  81.7 us (25%)
  starting transfers between devices  42.9 us (13%)
  matrix products  40.8 us (13%)
  local copies, waits for them, and re-layouts  10.5 us (3%)
  other arithmetic  5.31 us (2%)
    ppermute x20, waiting for transfers between devices, from_behind(): return lax.ppermute(shard, axis, pairs)  81.7 us
    psum x2, blocking collectives, coarse_term(): totals = lax.psum(placed, ('sx', 'sy'))  80.9 us
    ppermute x20, starting transfers between devices, from_behind(): return lax.ppermute(shard, axis, pairs)  42.9 us
    all_gather x2, blocking collectives, coarse_term(): lax.all_gather(solved, 'sx', axis=0, tiled=True)  30.1 us
    psum x2, blocking collectives, coarse_term(): solved = lax.psum(row_part, 'sy').astype(jnp.bfloat16)  26.7 us
    dot_general x5, matrix products, paired(): jnp.einsum('rsij,rsjl->rsil', wrinkle, vectors, preferred_element_type=jn...  21.4 us
    dot_general x5, matrix products, paired(): jnp.einsum('rsij,rsjl->rsil', taut, vectors, preferred_element_type=jnp.f...  16.1 us
  transfers between devices with their start and end apart: 20, of which 15 were waited for; matrix products, arithmetic and copies ran while one was open for 1% of the time, Pallas kernels for 0%

commit v1 on v0

--- a/solution.py
+++ b/solution.py
@@ -70,7 +70,8 @@
     )
     selector_float = selector.astype(jnp.float32)
     placed = jnp.einsum("kc,kl->cl", selector_float, corner_terms, precision=lax.Precision.HIGHEST)
-    totals = lax.psum(placed, ("sx", "sy"))
+    blocks = lax.all_gather(placed, ("sx", "sy"))
+    totals = jnp.sum(blocks, axis=0)
     column_part = lax.dynamic_slice_in_dim(totals, lax.axis_index("sy") * col_count, col_count, 0)
     row_part = jnp.dot(
         coarse_inverse, column_part.astype(jnp.bfloat16), preferred_element_type=jnp.float32

time: 321 us -> 369 us (1.15)
  waiting for transfers between devices: 81.7 us -> 196 us
  blocking collectives: 138 us -> 53.6 us
  between operations: 1.35 us -> 14.7 us
    all_gather x0 -> x2, waiting for transfers between devices: none -> 116 us  [coarse_term(): blocks = lax.all_gather(placed, ('sx', 'sy'))]
    psum x2 -> x0, blocking collectives: 80.9 us -> none  [coarse_term(): totals = lax.psum(placed, ('sx', 'sy'))]
    reduce_sum x0 -> x2, other arithmetic: none -> 4.79 us  [coarse_term(): totals = jnp.sum(blocks, axis=0)]
    all_gather x2, blocking collectives: 30.1 us -> 26.1 us  [coarse_term(): lax.all_gather(solved, 'sx', axis=0, tiled=True)]
  transfers between devices with their start and end apart: 20 -> 22, of which waited for: 15 -> 17; matrix products, arithmetic and copies ran while one was open for 1% -> 3% of each run, Pallas kernels for 0% -> 0%
where the time goes in v1:
time: 369 us; the launch traced here: 368 us
  waiting for transfers between devices  196 us (53%)
  blocking collectives  53.6 us (15%)
  matrix products  43.7 us (12%)
  starting transfers between devices  42.8 us (12%)
  between operations  14.7 us (4%)
  other arithmetic  8.77 us (2%)
  local copies, waits for them, and re-layouts  8.3 us (2%)
    all_gather x2, waiting for transfers between devices, coarse_term(): blocks = lax.all_gather(placed, ('sx', 'sy'))  116 us
    ppermute x20, waiting for transfers between devices, from_behind(): return lax.ppermute(shard, axis, pairs)  80.4 us
    ppermute x20, starting transfers between devices, from_behind(): return lax.ppermute(shard, axis, pairs)  42.7 us
    psum x2, blocking collectives, coarse_term(): solved = lax.psum(row_part, 'sy').astype(jnp.bfloat16)  27.5 us
    all_gather x2, blocking collectives, coarse_term(): lax.all_gather(solved, 'sx', axis=0, tiled=True)  26.1 us
    dot_general x5, matrix products, paired(): jnp.einsum('rsij,rsjl->rsil', wrinkle, vectors, preferred_element_type=jn...  21.1 us
    dot_general x5, matrix products, paired(): jnp.einsum('rsij,rsjl->rsil', taut, vectors, preferred_element_type=jnp.f...  18.6 us
  transfers between devices with their start and end apart: 22, of which 17 were waited for; matrix products, arithmetic and copies ran while one was open for 3% of the time, Pallas kernels for 0%

profile of v1, /device:TPU:1, one launch (start us, length us, event | category | flops | bytes accessed | tf_op | source)
XLA Modules:
  0.0 368.1 jit_solution(12246099008505629182)
XLA Ops:
  8.0 1.3 copy.33
  9.6 4.0 %collective-permute-start = (bf16[1,1,288,128]{2,3,1,0:T(8,128)(2,1)S(1)}, bf16[1,1,288,128]{2,3,1,0:T(8,128)(2,1)S(1)}, u32[]{:S(2)}, u32[]{:S(2)}) collective-permute-start(bf16[1,1,288,128]{2,3,1,0:T(8,128)(2,1)S(1)} %get-tuple-element.48), channel_id=1, source_target_pairs={{0,1},{1,2},{2,3},{4,5},{5,6},{6,7},{8,9},{9,10},{10,11},{12,13},{... | collective-permute-start | bytes 221192 | tf_op jit(solution)/shard_map/ppermute | solution.py:16
  13.6 4.0 %collective-permute-start.1 = (bf16[1,2,288,128]{2,3,1,0:T(8,128)(2,1)S(1)}, bf16[1,2,288,128]{2,3,1,0:T(8,128)(2,1)S(1)}, u32[]{:S(2)}, u32[]{:S(2)}) collective-permute-start(bf16[1,2,288,128]{2,3,1,0:T(8,128)(2,1)S(1)} %get-tuple-element.38), channel_id=1, source_target_pairs={{0,4},{4,8},{8,12},{12,16},{16,20},{20,24},{24,28},{1,5},{5,9},{9,... | collective-permute-start | bytes 442376 | tf_op jit(solution)/shard_map/ppermute | solution.py:16
  17.7 2.5 collective-permute-done.1
  20.8 4.3 %fusion.29 = f32[2,128,1152]{2,1,0:T(8,128)S(1)} fusion(bf16[1,2,1152,1152]{3,2,1,0:T(8,128)(2,1)} %param.14, bf16[1,2,1152,128]{2,3,1,0:T(8,128)(2,1)S(1)} %concatenate.138, f32[2]{0:T(128)S(1)} %convert_bitcast_fusion), kind=kOutput, calls=%fused_computation.23 | convolution fusion | flops 679772160 | bytes 7077896 | tf_op jit(solution)/shard_map/rsij,rsjl->rsil/dot_general | solution.py:56
  25.2 1.7 fusion.68
  28.3 5.1 %collective-permute-done.2 = f32[1,1,288,128]{2,3,1,0:T(8,128)S(1)} collective-permute-done((f32[1,1,288,128]{2,3,1,0:T(8,128)S(1)}, f32[1,1,288,128]{2,3,1,0:T(8,128)S(1)}, u32[]{:S(2)}, u32[]{:S(2)}) %collective-permute-start.2) | collective-permute-done | bytes 147488 | tf_op jit(solution)/shard_map/ppermute | solution.py:16
  33.6 1.9 collective-permute-start.3
  35.6 9.3 %collective-permute-done.3 = f32[1,2,288,128]{2,3,1,0:T(8,128)S(1)} collective-permute-done((f32[1,2,288,128]{2,3,1,0:T(8,128)S(1)}, f32[1,2,288,128]{2,3,1,0:T(8,128)S(1)}, u32[]{:S(2)}, u32[]{:S(2)}) %collective-permute-start.3) | collective-permute-done | bytes 294944 | tf_op jit(solution)/shard_map/ppermute | solution.py:16
  45.3 3.2 collective-permute-start.4
  48.5 2.0 collective-permute-start.5
  50.6 2.4 collective-permute-done.5
  55.1 4.2 %fusion.44 = f32[2,128,1152]{2,1,0:T(8,128)S(1)} fusion(bf16[1,2,1152,1152]{3,2,1,0:T(8,128)(2,1)} %param.12, bf16[1,2,1152,128]{2,3,1,0:T(8,128)(2,1)S(1)} %concatenate.141, f32[2]{0:T(128)S(1)} %convert_bitcast_fusion), kind=kOutput, calls=%fused_computation.28 | convolution fusion | flops 679772160 | bytes 7077896 | tf_op jit(solution)/shard_map/rsij,rsjl->rsil/dot_general | solution.py:56
  59.3 58.5 %all-gather.5.cloned.1.call-done = f32[8192,128]{1,0:T(8,128)} async-done(((f32[256,128]{1,0:T(8,128)}), f32[8192,128]{1,0:T(8,128)}) %all-gather.5.cloned.1.call-update) | async-done | bytes 4194320 | tf_op jit(solution)/shard_map/all_gather | solution.py:73
  117.8 2.4 reduce_sum.18
  120.3 13.8 %psum.14 = bf16[32,128]{1,0:T(8,128)(2,1)S(1)} all-reduce(f32[32,128]{1,0:T(8,128)S(1)} %convolution_bitcast_fusion.1), channel_id=1, replica_groups=mesh['sx'=8,'sy'=4] {'sy'}, use_global_device_ids=true, to_apply=%region_1.2 | all-reduce | flops 4096 | bytes 24576 | tf_op jit(solution)/shard_map/psum | solution.py:79
  134.1 13.1 %all_gather.20 = bf16[256,128]{1,0:T(8,128)(2,1)S(1)} all-gather(bf16[32,128]{1,0:T(8,128)(2,1)S(1)} %psum.14), channel_id=1, replica_groups=mesh['sx'=8,'sy'=4] {'sx'}, dimensions={0}, use_global_device_ids=true | all-gather | bytes 73728 | tf_op jit(solution)/shard_map/all_gather | solution.py:83
  147.7 4.2 %fusion.56 = f32[1,2,1152,128]{2,3,1,0:T(8,128)S(1)} fusion(f32[2,128,1152]{2,1,0:T(8,128)S(1)} %fusion.105, f32[2,128,1152]{2,1,0:T(8,128)S(1)} %fusion.44, bf16[1,2,1152,1152]{3,2,1,0:T(8,128)(2,1)} %param.11, bf16[1,2,1152,128]{2,3,1,0:T(8,128)(2,1)S(1)} %concatenate.141), kind=kOutput, calls=%fused_computation.32 | convolution fusion | flops 680067072 | bytes 9437184 | tf_op jit(solution)/shard_map/rsij,rsjl->rsil/dot_general | solution.py:55
  153.4 6.9 %collective-permute-done.6 = f32[1,1,288,128]{2,3,1,0:T(8,128)S(1)} collective-permute-done((f32[1,1,288,128]{2,3,1,0:T(8,128)S(1)}, f32[1,1,288,128]{2,3,1,0:T(8,128)S(1)}, u32[]{:S(2)}, u32[]{:S(2)}) %collective-permute-start.6) | collective-permute-done | bytes 147488 | tf_op jit(solution)/shard_map/ppermute | solution.py:16
  160.5 2.9 collective-permute-start.7
  163.4 6.2 %collective-permute-done.7 = f32[1,2,288,128]{2,3,1,0:T(8,128)S(1)} collective-permute-done((f32[1,2,288,128]{2,3,1,0:T(8,128)S(1)}, f32[1,2,288,128]{2,3,1,0:T(8,128)S(1)}, u32[]{:S(2)}, u32[]{:S(2)}) %collective-permute-start.7) | collective-permute-done | bytes 294944 | tf_op jit(solution)/shard_map/ppermute | solution.py:16
  171.3 1.9 collective-permute-start.9
  173.3 2.5 collective-permute-done.9
  176.4 4.2 %fusion.32 = f32[2,128,1152]{2,1,0:T(8,128)S(1)} fusion(bf16[1,2,1152,1152]{3,2,1,0:T(8,128)(2,1)} %param.14, bf16[1,2,1152,128]{2,3,1,0:T(8,128)(2,1)S(1)} %concatenate.144, f32[2]{0:T(128)S(1)} %convert_bitcast_fusion), kind=kOutput, calls=%fused_computation.24 | convolution fusion | flops 679772160 | bytes 7077896 | tf_op jit(solution)/shard_map/rsij,rsjl->rsil/dot_general | solution.py:56
  180.6 4.2 %fusion.65 = f32[1,2,1152,128]{2,3,1,0:T(8,128)S(1)} fusion(f32[2,128,1152]{2,1,0:T(8,128)S(1)} %fusion.32, bf16[1,2,1152,1152]{3,2,1,0:T(8,128)(2,1)} %param.13, bf16[1,2,1152,128]{2,3,1,0:T(8,128)(2,1)S(1)} %concatenate.144), kind=kOutput, calls=%fused_computation.35 | convolution fusion | flops 679772160 | bytes 8257536 | tf_op jit(solution)/shard_map/rsij,rsjl->rsil/dot_general | solution.py:55
  186.3 6.6 %collective-permute-done.10 = f32[1,1,288,128]{2,3,1,0:T(8,128)S(1)} collective-permute-done((f32[1,1,288,128]{2,3,1,0:T(8,128)S(1)}, f32[1,1,288,128]{2,3,1,0:T(8,128)S(1)}, u32[]{:S(2)}, u32[]{:S(2)}) %collective-permute-start.10) | collective-permute-done | bytes 147488 | tf_op jit(solution)/shard_map/ppermute | solution.py:16
  193.1 2.2 collective-permute-start.11
  195.3 7.5 %collective-permute-done.11 = f32[1,2,288,128]{2,3,1,0:T(8,128)S(1)} collective-permute-done((f32[1,2,288,128]{2,3,1,0:T(8,128)S(1)}, f32[1,2,288,128]{2,3,1,0:T(8,128)S(1)}, u32[]{:S(2)}, u32[]{:S(2)}) %collective-permute-start.11) | collective-permute-done | bytes 294944 | tf_op jit(solution)/shard_map/ppermute | solution.py:16
  204.2 2.6 collective-permute-start.12
  206.8 1.9 collective-permute-start.13
  208.8 2.5 collective-permute-done.13
  213.2 4.2 %fusion.47 = f32[2,128,1152]{2,1,0:T(8,128)S(1)} fusion(bf16[1,2,1152,1152]{3,2,1,0:T(8,128)(2,1)} %param.12, bf16[1,2,1152,128]{2,3,1,0:T(8,128)(2,1)S(1)} %concatenate.147, f32[2]{0:T(128)S(1)} %convert_bitcast_fusion), kind=kOutput, calls=%fused_computation.29 | convolution fusion | flops 679772160 | bytes 7077896 | tf_op jit(solution)/shard_map/rsij,rsjl->rsil/dot_general | solution.py:56
  217.4 57.3 %all-gather.7.cloned.1.call-done = f32[8192,128]{1,0:T(8,128)} async-done(((f32[256,128]{1,0:T(8,128)}), f32[8192,128]{1,0:T(8,128)}) %all-gather.7.cloned.1.call-update) | async-done | bytes 4194320 | tf_op jit(solution)/shard_map/all_gather | solution.py:73
  274.8 2.4 reduce_sum.19
  277.3 13.8 %psum.15 = bf16[32,128]{1,0:T(8,128)(2,1)S(1)} all-reduce(f32[32,128]{1,0:T(8,128)S(1)} %convolution_bitcast_fusion), channel_id=1, replica_groups=mesh['sx'=8,'sy'=4] {'sy'}, use_global_device_ids=true, to_apply=%region_3.4 | all-reduce | flops 4096 | bytes 24576 | tf_op jit(solution)/shard_map/psum | solution.py:79
  291.1 13.1 %all_gather.23 = bf16[256,128]{1,0:T(8,128)(2,1)S(1)} all-gather(bf16[32,128]{1,0:T(8,128)(2,1)S(1)} %psum.15), channel_id=1, replica_groups=mesh['sx'=8,'sy'=4] {'sx'}, dimensions={0}, use_global_device_ids=true | all-gather | bytes 73728 | tf_op jit(solution)/shard_map/all_gather | solution.py:83
  304.7 4.2 %fusion.59 = f32[1,2,1152,128]{2,3,1,0:T(8,128)S(1)} fusion(f32[2,128,1152]{2,1,0:T(8,128)S(1)} %fusion.102, f32[2,128,1152]{2,1,0:T(8,128)S(1)} %fusion.47, bf16[1,2,1152,1152]{3,2,1,0:T(8,128)(2,1)} %param.11, bf16[1,2,1152,128]{2,3,1,0:T(8,128)(2,1)S(1)} %concatenate.147), kind=kOutput, calls=%fused_computation.33 | convolution fusion | flops 680067072 | bytes 9437184 | tf_op jit(solution)/shard_map/rsij,rsjl->rsil/dot_general | solution.py:55
  310.4 6.9 %collective-permute-done.14 = f32[1,1,288,128]{2,3,1,0:T(8,128)S(1)} collective-permute-done((f32[1,1,288,128]{2,3,1,0:T(8,128)S(1)}, f32[1,1,288,128]{2,3,1,0:T(8,128)S(1)}, u32[]{:S(2)}, u32[]{:S(2)}) %collective-permute-start.14) | collective-permute-done | bytes 147488 | tf_op jit(solution)/shard_map/ppermute | solution.py:16
  317.5 2.9 collective-permute-start.15
  320.4 6.2 %collective-permute-done.15 = f32[1,2,288,128]{2,3,1,0:T(8,128)S(1)} collective-permute-done((f32[1,2,288,128]{2,3,1,0:T(8,128)S(1)}, f32[1,2,288,128]{2,3,1,0:T(8,128)S(1)}, u32[]{:S(2)}, u32[]{:S(2)}) %collective-permute-start.15) | collective-permute-done | bytes 294944 | tf_op jit(solution)/shard_map/ppermute | solution.py:16
  328.3 1.9 collective-permute-start.17
  330.3 2.5 collective-permute-done.17
  333.4 4.2 %fusion.35 = f32[2,128,1152]{2,1,0:T(8,128)S(1)} fusion(bf16[1,2,1152,1152]{3,2,1,0:T(8,128)(2,1)} %param.14, bf16[1,2,1152,128]{2,3,1,0:T(8,128)(2,1)S(1)} %concatenate.150, f32[2]{0:T(128)S(1)} %convert_bitcast_fusion), kind=kOutput, calls=%fused_computation.25 | convolution fusion | flops 679772160 | bytes 7077896 | tf_op jit(solution)/shard_map/rsij,rsjl->rsil/dot_general | solution.py:56
  337.6 4.2 %fusion.62 = f32[1,2,1152,128]{2,3,1,0:T(8,128)S(1)} fusion(f32[2,128,1152]{2,1,0:T(8,128)S(1)} %fusion.35, bf16[1,2,1152,1152]{3,2,1,0:T(8,128)(2,1)} %param.13, bf16[1,2,1152,128]{2,3,1,0:T(8,128)(2,1)S(1)} %concatenate.150), kind=kOutput, calls=%fused_computation.34 | convolution fusion | flops 679772160 | bytes 8257536 | tf_op jit(solution)/shard_map/rsij,rsjl->rsil/dot_general | solution.py:55
  342.0 1.4 collective-permute-start.18
  343.4 6.6 %collective-permute-done.18 = f32[1,1,288,128]{2,3,1,0:T(8,128)S(1)} collective-permute-done((f32[1,1,288,128]{2,3,1,0:T(8,128)S(1)}, f32[1,1,288,128]{2,3,1,0:T(8,128)S(1)}, u32[]{:S(2)}, u32[]{:S(2)}) %collective-permute-start.18) | collective-permute-done | bytes 147488 | tf_op jit(solution)/shard_map/ppermute | solution.py:16
  350.2 2.0 collective-permute-start.19
  353.3 6.6 %collective-permute-done.19 = f32[1,2,288,128]{2,3,1,0:T(8,128)S(1)} collective-permute-done((f32[1,2,288,128]{2,3,1,0:T(8,128)S(1)}, f32[1,2,288,128]{2,3,1,0:T(8,128)S(1)}, u32[]{:S(2)}, u32[]{:S(2)}) %collective-permute-start.19) | collective-permute-done | bytes 294944 | tf_op jit(solution)/shard_map/ppermute | solution.py:16
  (95 shorter events, 22.8 us)
Async XLA Ops:
  7.2 46.5 %copy-start = (bf16[1,2,12,1152]{3,1,2,0:T(2,128)(2,1)S(1)}, bf16[1,2,12,1152]{3,1,2,0:T(2,128)(2,1)}, u32[]{:S(2)}) copy-start(bf16[1,2,12,1152]{3,1,2,0:T(2,128)(2,1)} %param.15) | copy-start | bytes 165892
  7.2 110.6 %all-gather.5.cloned.1.call-start = ((), (), s32[]{:S(2)}) async-start(), calls=%async_computation | async-start | bytes 4325376 | tf_op jit(solution)/shard_map/all_gather | solution.py:73
  9.4 8.2 %copy-start.5 = (s32[1,2]{1,0:T(1,128)S(1)}, s32[1,2]{1,0:T(1,128)}, u32[]{:S(2)}) copy-start(s32[1,2]{1,0:T(1,128)} %param.17) | copy-start | bytes 28
  9.6 8.0 %collective-permute-start = (bf16[1,1,288,128]{2,3,1,0:T(8,128)(2,1)S(1)}, bf16[1,1,288,128]{2,3,1,0:T(8,128)(2,1)S(1)}, u32[]{:S(2)}, u32[]{:S(2)}) collective-permute-start(bf16[1,1,288,128]{2,3,1,0:T(8,128)(2,1)S(1)} %get-tuple-element.48), channel_id=1, source_target_pairs={{0,1},{1,2},{2,3},{4,5},{5,6},{6,7},{8,9},{9,10},{10,11},{12,13},{... | collective-permute-start | bytes 221192 | tf_op jit(solution)/shard_map/ppermute | solution.py:16
  13.6 6.6 %collective-permute-start.1 = (bf16[1,2,288,128]{2,3,1,0:T(8,128)(2,1)S(1)}, bf16[1,2,288,128]{2,3,1,0:T(8,128)(2,1)S(1)}, u32[]{:S(2)}, u32[]{:S(2)}) collective-permute-start(bf16[1,2,288,128]{2,3,1,0:T(8,128)(2,1)S(1)} %get-tuple-element.38), channel_id=1, source_target_pairs={{0,4},{4,8},{8,12},{12,16},{16,20},{20,24},{24,28},{1,5},{5,9},{9,... | collective-permute-start | bytes 442376 | tf_op jit(solution)/shard_map/ppermute | solution.py:16
  20.8 4.4 %copy-start.1 = (bf16[1,2,1152,1152]{3,2,1,0:T(8,128)(2,1)S(1)}, bf16[1,2,1152,1152]{3,2,1,0:T(8,128)(2,1)}, u32[]{:S(2)}) copy-start(bf16[1,2,1152,1152]{3,2,1,0:T(8,128)(2,1)} %param.13) | copy-start | bytes 15925252
  27.0 6.4 %collective-permute-start.2 = (f32[1,1,288,128]{2,3,1,0:T(8,128)S(1)}, f32[1,1,288,128]{2,3,1,0:T(8,128)S(1)}, u32[]{:S(2)}, u32[]{:S(2)}) collective-permute-start(f32[1,1,288,128]{2,3,1,0:T(8,128)S(1)} %get-tuple-element.29), channel_id=1, source_target_pairs={{1,0},{2,1},{3,2},{5,4},{6,5},{7,6},{9,8},{10,9},{11,10},{13,12},{... | collective-permute-start | bytes 442376 | tf_op jit(solution)/shard_map/ppermute | solution.py:16
  33.6 11.3 %collective-permute-start.3 = (f32[1,2,288,128]{2,3,1,0:T(8,128)S(1)}, f32[1,2,288,128]{2,3,1,0:T(8,128)S(1)}, u32[]{:S(2)}, u32[]{:S(2)}) collective-permute-start(f32[1,2,288,128]{2,3,1,0:T(8,128)S(1)} %get-tuple-element.27), channel_id=1, source_target_pairs={{4,0},{8,4},{12,8},{16,12},{20,16},{24,20},{28,24},{5,1},{9,5},{13... | collective-permute-start | bytes 884744 | tf_op jit(solution)/shard_map/ppermute | solution.py:16
  45.1 5.4 %copy-start.4 = (s32[1,2,12]{2,1,0:T(2,128)S(1)}, s32[1,2,12]{2,1,0:T(2,128)}, u32[]{:S(2)}) copy-start(s32[1,2,12]{2,1,0:T(2,128)} %param.19) | copy-start | bytes 292
  45.3 5.3 %collective-permute-start.4 = (bf16[1,1,288,128]{2,3,1,0:T(8,128)(2,1)S(1)}, bf16[1,1,288,128]{2,3,1,0:T(8,128)(2,1)S(1)}, u32[]{:S(2)}, u32[]{:S(2)}) collective-permute-start(bf16[1,1,288,128]{2,3,1,0:T(8,128)(2,1)S(1)} %get-tuple-element.46), channel_id=1, source_target_pairs={{0,1},{1,2},{2,3},{4,5},{5,6},{6,7},{8,9},{9,10},{10,11},{12,13},{... | collective-permute-start | bytes 221192 | tf_op jit(solution)/shard_map/ppermute | solution.py:16
  48.5 4.6 %collective-permute-start.5 = (bf16[1,2,288,128]{2,3,1,0:T(8,128)(2,1)S(1)}, bf16[1,2,288,128]{2,3,1,0:T(8,128)(2,1)S(1)}, u32[]{:S(2)}, u32[]{:S(2)}) collective-permute-start(bf16[1,2,288,128]{2,3,1,0:T(8,128)(2,1)S(1)} %get-tuple-element.36), channel_id=1, source_target_pairs={{0,4},{4,8},{8,12},{12,16},{16,20},{20,24},{24,28},{1,5},{5,9},{9,... | collective-permute-start | bytes 442376 | tf_op jit(solution)/shard_map/ppermute | solution.py:16
  55.0 219.7 %all-gather.7.cloned.1.call-start = ((), (), s32[]{:S(2)}) async-start(), calls=%async_computation.1 | async-start | bytes 4325376 | tf_op jit(solution)/shard_map/all_gather | solution.py:73
  117.8 2.4 copy-start.3
  152.1 8.2 %collective-permute-start.6 = (f32[1,1,288,128]{2,3,1,0:T(8,128)S(1)}, f32[1,1,288,128]{2,3,1,0:T(8,128)S(1)}, u32[]{:S(2)}, u32[]{:S(2)}) collective-permute-start(f32[1,1,288,128]{2,3,1,0:T(8,128)S(1)} %get-tuple-element.25), channel_id=1, source_target_pairs={{1,0},{2,1},{3,2},{5,4},{6,5},{7,6},{9,8},{10,9},{11,10},{13,12},{... | collective-permute-start | bytes 442376 | tf_op jit(solution)/shard_map/ppermute | solution.py:16
  160.5 9.1 %collective-permute-start.7 = (f32[1,2,288,128]{2,3,1,0:T(8,128)S(1)}, f32[1,2,288,128]{2,3,1,0:T(8,128)S(1)}, u32[]{:S(2)}, u32[]{:S(2)}) collective-permute-start(f32[1,2,288,128]{2,3,1,0:T(8,128)S(1)} %get-tuple-element.23), channel_id=1, source_target_pairs={{4,0},{8,4},{12,8},{16,12},{20,16},{24,20},{28,24},{5,1},{9,5},{13... | collective-permute-start | bytes 884744 | tf_op jit(solution)/shard_map/ppermute | solution.py:16
  170.0 3.2 collective-permute-start.8
  171.3 4.5 %collective-permute-start.9 = (bf16[1,2,288,128]{2,3,1,0:T(8,128)(2,1)S(1)}, bf16[1,2,288,128]{2,3,1,0:T(8,128)(2,1)S(1)}, u32[]{:S(2)}, u32[]{:S(2)}) collective-permute-start(bf16[1,2,288,128]{2,3,1,0:T(8,128)(2,1)S(1)} %get-tuple-element.34), channel_id=1, source_target_pairs={{0,4},{4,8},{8,12},{12,16},{16,20},{20,24},{24,28},{1,5},{5,9},{9,... | collective-permute-start | bytes 442376 | tf_op jit(solution)/shard_map/ppermute | solution.py:16
  185.0 7.9 %collective-permute-start.10 = (f32[1,1,288,128]{2,3,1,0:T(8,128)S(1)}, f32[1,1,288,128]{2,3,1,0:T(8,128)S(1)}, u32[]{:S(2)}, u32[]{:S(2)}) collective-permute-start(f32[1,1,288,128]{2,3,1,0:T(8,128)S(1)} %get-tuple-element.21), channel_id=1, source_target_pairs={{1,0},{2,1},{3,2},{5,4},{6,5},{7,6},{9,8},{10,9},{11,10},{13,12},{... | collective-permute-start | bytes 442376 | tf_op jit(solution)/shard_map/ppermute | solution.py:16
  193.1 9.7 %collective-permute-start.11 = (f32[1,2,288,128]{2,3,1,0:T(8,128)S(1)}, f32[1,2,288,128]{2,3,1,0:T(8,128)S(1)}, u32[]{:S(2)}, u32[]{:S(2)}) collective-permute-start(f32[1,2,288,128]{2,3,1,0:T(8,128)S(1)} %get-tuple-element.19), channel_id=1, source_target_pairs={{4,0},{8,4},{12,8},{16,12},{20,16},{24,20},{28,24},{5,1},{9,5},{13... | collective-permute-start | bytes 884744 | tf_op jit(solution)/shard_map/ppermute | solution.py:16
  204.2 4.5 %collective-permute-start.12 = (bf16[1,1,288,128]{2,3,1,0:T(8,128)(2,1)S(1)}, bf16[1,1,288,128]{2,3,1,0:T(8,128)(2,1)S(1)}, u32[]{:S(2)}, u32[]{:S(2)}) collective-permute-start(bf16[1,1,288,128]{2,3,1,0:T(8,128)(2,1)S(1)} %get-tuple-element.42), channel_id=1, source_target_pairs={{0,1},{1,2},{2,3},{4,5},{5,6},{6,7},{8,9},{9,10},{10,11},{12,13},{... | collective-permute-start | bytes 221192 | tf_op jit(solution)/shard_map/ppermute | solution.py:16
  206.8 4.5 %collective-permute-start.13 = (bf16[1,2,288,128]{2,3,1,0:T(8,128)(2,1)S(1)}, bf16[1,2,288,128]{2,3,1,0:T(8,128)(2,1)S(1)}, u32[]{:S(2)}, u32[]{:S(2)}) collective-permute-start(bf16[1,2,288,128]{2,3,1,0:T(8,128)(2,1)S(1)} %get-tuple-element.32), channel_id=1, source_target_pairs={{0,4},{4,8},{8,12},{12,16},{16,20},{20,24},{24,28},{1,5},{5,9},{9,... | collective-permute-start | bytes 442376 | tf_op jit(solution)/shard_map/ppermute | solution.py:16
  309.1 8.2 %collective-permute-start.14 = (f32[1,1,288,128]{2,3,1,0:T(8,128)S(1)}, f32[1,1,288,128]{2,3,1,0:T(8,128)S(1)}, u32[]{:S(2)}, u32[]{:S(2)}) collective-permute-start(f32[1,1,288,128]{2,3,1,0:T(8,128)S(1)} %get-tuple-element.17), channel_id=1, source_target_pairs={{1,0},{2,1},{3,2},{5,4},{6,5},{7,6},{9,8},{10,9},{11,10},{13,12},{... | collective-permute-start | bytes 442376 | tf_op jit(solution)/shard_map/ppermute | solution.py:16
  317.5 9.1 %collective-permute-start.15 = (f32[1,2,288,128]{2,3,1,0:T(8,128)S(1)}, f32[1,2,288,128]{2,3,1,0:T(8,128)S(1)}, u32[]{:S(2)}, u32[]{:S(2)}) collective-permute-start(f32[1,2,288,128]{2,3,1,0:T(8,128)S(1)} %get-tuple-element.15), channel_id=1, source_target_pairs={{4,0},{8,4},{12,8},{16,12},{20,16},{24,20},{28,24},{5,1},{9,5},{13... | collective-permute-start | bytes 884744 | tf_op jit(solution)/shard_map/ppermute | solution.py:16
  327.0 3.2 collective-permute-start.16
  328.3 4.5 %collective-permute-start.17 = (bf16[1,2,288,128]{2,3,1,0:T(8,128)(2,1)S(1)}, bf16[1,2,288,128]{2,3,1,0:T(8,128)(2,1)S(1)}, u32[]{:S(2)}, u32[]{:S(2)}) collective-permute-start(bf16[1,2,288,128]{2,3,1,0:T(8,128)(2,1)S(1)} %get-tuple-element.30), channel_id=1, source_target_pairs={{0,4},{4,8},{8,12},{12,16},{16,20},{20,24},{24,28},{1,5},{5,9},{9,... | collective-permute-start | bytes 442376 | tf_op jit(solution)/shard_map/ppermute | solution.py:16
  342.0 10.2 %copy-start.2 = (f32[1,2,2,288,128]{3,4,1,2,0:T(8,128)S(1)}, f32[1,2,2,288,128]{3,4,1,2,0:T(8,128)}, u32[]{:S(2)}) copy-start(f32[1,2,2,288,128]{3,4,1,2,0:T(8,128)} %get-tuple-element.9) | copy-start | bytes 1769476
  342.0 8.1 %collective-permute-start.18 = (f32[1,1,288,128]{2,3,1,0:T(8,128)S(1)}, f32[1,1,288,128]{2,3,1,0:T(8,128)S(1)}, u32[]{:S(2)}, u32[]{:S(2)}) collective-permute-start(f32[1,1,288,128]{2,3,1,0:T(8,128)S(1)} %get-tuple-element.13), channel_id=1, source_target_pairs={{1,0},{2,1},{3,2},{5,4},{6,5},{7,6},{9,8},{10,9},{11,10},{13,12},{... | collective-permute-start | bytes 442376 | tf_op jit(solution)/shard_map/ppermute | solution.py:16
  350.2 9.7 %collective-permute-start.19 = (f32[1,2,288,128]{2,3,1,0:T(8,128)S(1)}, f32[1,2,288,128]{2,3,1,0:T(8,128)S(1)}, u32[]{:S(2)}, u32[]{:S(2)}) collective-permute-start(f32[1,2,288,128]{2,3,1,0:T(8,128)S(1)} %get-tuple-element.11), channel_id=1, source_target_pairs={{4,0},{8,4},{12,8},{16,12},{20,16},{24,20},{28,24},{5,1},{9,5},{13... | collective-permute-start | bytes 884744 | tf_op jit(solution)/shard_map/ppermute | solution.py:16
Sparse Core Ops, SparseCore 0:
  55.2 62.5 all-gather.4
  213.4 61.3 all-gather.6
